TPU v7x, 32 devices: a whole 2x2x4 slice. The times are simulated.
32 devices in a mesh: tm: 16 (over z, x, core), space: 2 (over y).
Axes of the slice: x: 2, y: 2, z: 4, core: 2. Of those that a mesh axis runs over, the one named last changes fastest.
Arguments:
- snapshots: bfloat16 [512, 5, 4096], P('tm', None, 'space'), may hold values from -210 to 210, as said below
- basis: bfloat16 [2, 33, 16, 5, 4096], P(None, None, None, None, ('space', 'tm')), may hold values from -6 to 6
- mass_table: float32 [8, 64, 64], replicated, may hold values from -0.03 to 3, as said below
- elem_kind: int32 [64], P(('space', 'tm')), may hold values from 0 to 7
- offsets: int32 [8], replicated, may hold values from 0 to 256, as said below
Outputs:
- coeffs: float32 [2, 33, 8, 16], replicated
- new_basis: bfloat16 [2, 33, 16, 5, 4096], P(None, None, None, None, ('space', 'tm'))
Inputs may be any that keep to these rules, and one draw needn't show every extreme that they name: `snapshots`: rows of flow data. `mass_table`: each block is symmetric and positive definite. `offsets`: some block starts at 0 and some at 256.
All inputs are finite; a program needn't handle non-finite values.
Results may differ from a plain program's by a relative error of at most 0.0095.
Values may be sent and summed in bfloat16 or wider, within the bound.
A program may use at most 64 MiB of HBM per device.

v0:
```python
import math
import jax
import jax.numpy as jnp
from jax import lax
from jax.sharding import PartitionSpec as P

NT = 256


def spectral_table(offsets, window_len, freq_count, record_len):
    snap_idx = jnp.arange(record_len, dtype=jnp.int32)
    time_lag = snap_idx[None, :] - offsets[:, None]
    inside = (time_lag >= 0) & (time_lag < window_len)
    lag_clip = jnp.clip(time_lag, 0, window_len - 1)
    lag_float = lag_clip.astype(jnp.float32)
    hann_wt = 0.5 - 0.5 * jnp.cos(2.0 * math.pi / window_len * lag_float)
    norm_wt = 1.0 / math.sqrt(0.375 * window_len)
    freq_idx = jnp.arange(freq_count, dtype=jnp.int32)
    phase_int = jnp.mod(freq_idx[:, None, None] * lag_clip[None], window_len)
    angle = 2.0 * math.pi / window_len * phase_int.astype(jnp.float32)
    weight = jnp.where(inside, hann_wt * norm_wt, jnp.zeros_like(hann_wt))[None]
    real_part = weight * jnp.cos(angle)
    imag_part = -weight * jnp.sin(angle)
    return jnp.stack([real_part, imag_part]).astype(jnp.bfloat16)


def apply_mass(field, local_mass):
    lead = field.shape[:-1]
    elem_count = local_mass.shape[0]
    shaped = field.reshape(lead + (elem_count, local_mass.shape[1]))
    result = jnp.einsum("...ep,epq->...eq", shaped, local_mass, precision=lax.Precision.HIGHEST)
    return result.reshape(field.shape)


def paired_einsum(pattern, first_pair, second_pair):
    real_out = jnp.einsum(
        pattern, first_pair[0], second_pair[0], preferred_element_type=jnp.float32
    ) + jnp.einsum(pattern, first_pair[1], second_pair[1], preferred_element_type=jnp.float32)
    imag_out = jnp.einsum(
        pattern, first_pair[0], second_pair[1], preferred_element_type=jnp.float32
    ) - jnp.einsum(pattern, first_pair[1], second_pair[0], preferred_element_type=jnp.float32)
    return (real_out, imag_out)


def on_device(snapshots, basis, mass_table, elem_kind, offsets):
    regrouped = lax.all_to_all(snapshots, "tm", split_axis=2, concat_axis=0, tiled=True)
    record_len, var_count, local_pts = regrouped.shape
    freq_count = basis.shape[1]
    mode_count = basis.shape[2]
    block_total = offsets.shape[0]
    kind_count = mass_table.shape[0]
    flat_len = var_count * local_pts
    entries = flat_len * lax.axis_size("tm") * lax.axis_size("space")
    dft_table = spectral_table(offsets, NT, freq_count, record_len)
    record_flat = regrouped.reshape(record_len, flat_len)
    spectra = jnp.dot(
        dft_table.reshape(2 * freq_count * block_total, record_len),
        record_flat,
        preferred_element_type=jnp.float32,
    )
    selector = (elem_kind[:, None] == jnp.arange(kind_count, dtype=jnp.int32)[None, :]).astype(
        jnp.float32
    )
    local_mass = jnp.einsum("ek,kpq->epq", selector, mass_table, precision=lax.Precision.HIGHEST)
    spectra = spectra.reshape(2, freq_count, block_total, var_count, local_pts)
    weighted = (
        apply_mass(spectra, local_mass)
        .astype(jnp.bfloat16)
        .reshape(2, freq_count, block_total, flat_len)
    )
    mode_rows = basis.reshape(2, freq_count, mode_count, flat_len)
    coeff_real, coeff_imag = paired_einsum("fkx,fbx->fbk", mode_rows, weighted)
    coeff_part = jnp.stack([coeff_real, coeff_imag])
    spec_round = spectra.astype(jnp.bfloat16).reshape(2, freq_count, block_total, flat_len)
    gram_real, gram_imag = paired_einsum("fbx,fcx->fbc", spec_round, weighted)
    coeff_sum, gram_real, gram_imag = lax.psum((coeff_part, gram_real, gram_imag), ("tm", "space"))
    coeffs = coeff_sum / math.sqrt(entries)
    table_float = dft_table.astype(jnp.float32)
    coeff_round = lax.optimization_barrier(coeffs.astype(jnp.bfloat16)).astype(jnp.float32)
    kernel_real = jnp.einsum("fbt,fbk->fkt", table_float[0], coeff_round[0]) - jnp.einsum(
        "fbt,fbk->fkt", table_float[1], coeff_round[1]
    )
    kernel_imag = jnp.einsum("fbt,fbk->fkt", table_float[0], coeff_round[1]) + jnp.einsum(
        "fbt,fbk->fkt", table_float[1], coeff_round[0]
    )
    kernel = (
        jnp.stack([kernel_real, kernel_imag])
        .astype(jnp.bfloat16)
        .reshape(2 * freq_count * mode_count, record_len)
    )
    fields = jnp.dot(kernel, record_flat, preferred_element_type=jnp.float32)
    fields = fields.reshape(2, freq_count, mode_count, var_count, local_pts)
    apply_real = jnp.einsum("fbc,fck->fbk", gram_real, coeff_round[0]) - jnp.einsum(
        "fbc,fck->fbk", gram_imag, coeff_round[1]
    )
    apply_imag = jnp.einsum("fbc,fck->fbk", gram_real, coeff_round[1]) + jnp.einsum(
        "fbc,fck->fbk", gram_imag, coeff_round[0]
    )
    energy = jnp.sum(coeff_round[0] * apply_real + coeff_round[1] * apply_imag, axis=1)
    factor = 1.0 / jnp.sqrt(energy / entries + 1e-06)
    new_basis = (fields * factor[None, :, :, None, None]).astype(jnp.bfloat16)
    return (coeffs, new_basis)


def solution(mesh):
    return jax.shard_map(
        on_device,
        mesh=mesh,
        in_specs=(
            P("tm", None, "space"),
            P(None, None, None, None, ("space", "tm")),
            P(),
            P(("space", "tm")),
            P(),
        ),
        out_specs=(P(), P(None, None, None, None, ("space", "tm"))),
        check_vma=False,
    )
```

profile of v0, /device:TPU:0, one launch (start us, length us, event | category | flops | bytes accessed | tf_op | source)
XLA Modules:
  0.0 120.1 jit_solution(16826947783138899716)
XLA Ops:
  0.6 0.0 copy-start
  0.6 5.4 %copy.35 = bf16[32,5,2048]{0,1,2:T(8,128)(2,1)} copy(bf16[32,5,2048]{2,0,1:T(8,128)(2,1)} %param.5) | data formatting | bytes 1310720 | tf_op args[0]
  6.0 0.0 copy-start.6
  6.0 5.2 %reshape.176 = bf16[16,2,10240]{2,1,0:T(2,128)(2,1)} reshape(bf16[2048,5,32]{2,1,0:T(8,128)(2,1)} %bitcast.99) | data formatting | bytes 1310720
  11.3 7.4 %all-to-all-start = ((bf16[16,2,10240]{2,1,0:T(2,128)(2,1)}), bf16[16,2,10240]{2,1,0:T(2,128)(2,1)S(1)}, u32[]{:S(2)}, u32[]{:S(2)}) async-start(bf16[16,2,10240]{2,1,0:T(2,128)(2,1)} %reshape.176), calls=%async_computation | async-start | bytes 1310720 | tf_op jit(solution)/shard_map/all_to_all | solution.py:46
  18.6 0.0 copy-done.6
  18.7 0.2 fusion.69
  18.9 0.3 copy.40
  19.2 1.6 %squeeze.25 = bf16[33,16,640]{2,1,0:T(8,128)(2,1)} reshape(bf16[1,33,16,5,128]{4,3,2,1,0:T(8,128)(2,1)S(1)} %copy.40) | data formatting | bytes 1351680 | tf_op jit(solution)/shard_map/squeeze | solution.py:37
  20.8 0.0 copy-start.8
  20.8 0.3 copy.42
  21.1 0.0 copy-start.7
  21.1 1.7 %squeeze.27 = bf16[33,16,640]{2,1,0:T(8,128)(2,1)} reshape(bf16[1,33,16,5,128]{4,3,2,1,0:T(8,128)(2,1)S(1)} %copy.42) | data formatting | bytes 1351680 | tf_op jit(solution)/shard_map/squeeze | solution.py:38
  22.8 0.0 copy-done
  22.8 0.0 copy-done.8
  22.8 0.4 convolution_bitcast_fusion
  23.2 0.0 copy-done.7
  23.2 0.1 fusion.42
  23.3 0.1 multiply_select_fusion
  23.4 2.2 %multiply_convert_fusion.2 = (bf16[1,33,8,512]{3,2,1,0:T(8,128)(2,1)S(1)}, bf16[1,33,8,512]{3,2,1,0:T(8,128)(2,1)S(1)}) fusion(s32[8,512]{1,0:T(8,128)S(1)} %fusion.42, f32[8,512]{1,0:T(8,128)S(1)} %get-tuple-element.21, f32[8,512]{1,0:T(8,128)S(1)} %get-tuple-element.22), kind=kLoop, calls=%fused_computation.38 | loop fusion | flops 2433024 | bytes 589824 | tf_op jit(solution)/shard_map/slice | solution.py:80
  25.7 0.1 pad_maximum_fusion
  25.7 9.5 %all-to-all-done = bf16[16,2,10240]{2,1,0:T(2,128)(2,1)S(1)} async-done(((bf16[16,2,10240]{2,1,0:T(2,128)(2,1)}), bf16[16,2,10240]{2,1,0:T(2,128)(2,1)S(1)}, u32[]{:S(2)}, u32[]{:S(2)}) %all-to-all-start) | async-done | bytes 655392 | tf_op jit(solution)/shard_map/all_to_all | solution.py:46
  35.2 4.0 %reshape.177 = bf16[2048,5,32]{2,1,0:T(8,128)(2,1)} reshape(bf16[16,2,10240]{2,1,0:T(2,128)(2,1)S(1)} %all-to-all-done) | data formatting | bytes 1310720
  39.2 4.5 %copy.36 = bf16[32,5,16,128]{3,1,0,2:T(8,128)(2,1)S(1)} copy(bf16[32,5,16,128]{0,1,3,2:T(8,128)(2,1)} %bitcast.98) | data formatting | bytes 1310720 | tf_op jit(solution)/shard_map/all_to_all | solution.py:46
  43.6 0.0 copy-start.1
  43.7 1.9 %fusion.70 = (bf16[528,640]{1,0:T(8,128)(2,1)}, f32[528,640]{1,0:T(8,128)}) fusion(bf16[528,512]{1,0:T(8,128)(2,1)S(1)} %bitcast.103, bf16[64,8,5,128]{3,2,1,0:T(8,128)(2,1)S(1)} %bitcast.100), kind=kOutput, calls=%fused_computation.95 | convolution fusion | flops 346368000 | bytes 3223552 | tf_op jit(solution)/shard_map/dot_general | solution.py:56
  45.6 0.0 copy-done.1
  45.6 3.1 %reshape_reshape.3 = f32[2,33,8,5,2,64]{5,4,3,2,1,0:T(2,128)S(1)} reshape(f32[528,640]{1,0:T(8,128)} %get-tuple-element.24) | data formatting | bytes 2703360 | tf_op jit(solution)/shard_map/reshape;reshape | solution.py:30
  48.7 3.5 %fusion.5 = bf16[2,33,8,5,2,64]{5,1,3,2,0,4:T(8,128)(2,1)S(1)} fusion(f32[2,33,8,5,2,64]{5,4,3,2,1,0:T(2,128)S(1)} %reshape_reshape.3, f32[2,64,64,1,1,1]{2,0,1,5,4,3:T(2,128)S(1)} %convolution_bitcast_fusion), kind=kOutput, calls=%fused_computation.4 | convolution fusion | flops 259860480 | bytes 2060288 | tf_op jit(solution)/shard_map/...ep,epq->...eq/dot_general | solution.py:31
  52.2 0.3 fusion.68
  52.5 0.7 copy.41
  53.2 0.4 squeeze.26
  53.6 0.0 copy-start.5
  53.6 0.7 copy.39
  54.3 0.0 copy-start.4
  54.3 0.4 squeeze.24
  54.7 0.0 copy-done.5
  54.8 0.3 fusion.36
  55.1 0.3 fusion.37
  55.4 0.1 copy-done.4
  55.5 0.4 fusion.71
  55.9 0.0 copy-start.3
  55.9 0.4 fusion.72
  56.2 0.4 convolution_subtract_fusion.1
  56.6 0.3 convolution_add_fusion.1
  56.9 0.1 copy-done.3
  57.0 0.3 fusion.16
  57.3 0.4 fusion.15
  57.7 48.1 %all-reduce = (f32[2,33,8,16]{3,2,1,0:T(8,128)S(1)}, bf16[33,8,8]{2,1,0:T(8,128)(2,1)S(1)}, bf16[33,8,8]{2,1,0:T(8,128)(2,1)S(1)}) all-reduce(f32[2,33,8,16]{3,2,1,0:T(8,128)S(1)} %pad_maximum_fusion.1, f32[33,8,8]{2,1,0:T(8,128)S(1)} %convolution_add_fusion.1, ...), channel_id=1, replica_groups=mesh['tm'=16,'space'=2] {'tm','space'}, use_global_device_ids=true, to_apply=%region_0.1 | all-reduce | flops 12672 | bytes 92928 | tf_op jit(solution)/shard_map/psum | solution.py:76
  105.9 2.0 %fusion.33 = f32[33,16,512]{2,1,0:T(8,128)S(1)} fusion(s32[8,512]{1,0:T(8,128)S(1)} %fusion.42, f32[8,512]{1,0:T(8,128)S(1)} %get-tuple-element.21, bf16[2,33,8,16]{3,2,1,0:T(8,128)(2,1)S(1)} %get-tuple-element.17), kind=kOutput, calls=%fused_computation.50 | convolution fusion | flops 6488064 | bytes 1181696 | tf_op jit(solution)/shard_map/fbt,fbk->fkt/dot_general | solution.py:80
  107.9 2.0 %fusion.31 = f32[33,16,512]{2,1,0:T(8,128)S(1)} fusion(s32[8,512]{1,0:T(8,128)S(1)} %fusion.42, f32[8,512]{1,0:T(8,128)S(1)} %get-tuple-element.21, bf16[2,33,8,16]{3,2,1,0:T(8,128)(2,1)S(1)} %get-tuple-element.17), kind=kOutput, calls=%fused_computation.48 | convolution fusion | flops 6488064 | bytes 1181696 | tf_op jit(solution)/shard_map/fbt,fbk->fkt/dot_general | solution.py:83
  110.0 0.2 fusion.39
  110.1 0.2 fusion.40
  110.3 0.0 copy-done.2
  110.4 0.1 copy.68
  110.5 3.0 %fusion.11 = bf16[1,33,16,512]{3,2,1,0:T(8,128)(2,1)} fusion(f32[33,16,512]{2,1,0:T(8,128)S(1)} %fusion.33, f32[8,512]{1,0:T(8,128)S(1)} %get-tuple-element.22, s32[8,512]{1,0:T(8,128)S(1)} %fusion.42, bf16[2,33,8,16]{3,2,1,0:T(8,128)(2,1)S(1)} %get-tuple-element.17), kind=kOutput, calls=%fused_computation.10 | convolution fusion | flops 7028736 | bytes 1722368 | tf_op jit(solution)/shard_map/fbt,fbk->fkt/dot_general | solution.py:80
  113.5 3.0 %fusion.10 = bf16[1,33,16,512]{3,2,1,0:T(8,128)(2,1)} fusion(f32[33,16,512]{2,1,0:T(8,128)S(1)} %fusion.31, f32[8,512]{1,0:T(8,128)S(1)} %get-tuple-element.22, s32[8,512]{1,0:T(8,128)S(1)} %fusion.42, bf16[2,33,8,16]{3,2,1,0:T(8,128)(2,1)S(1)} %get-tuple-element.17), kind=kOutput, calls=%fused_computation.9 | convolution fusion | flops 7028736 | bytes 1722368 | tf_op jit(solution)/shard_map/fbt,fbk->fkt/dot_general | solution.py:83
  116.5 0.2 fusion.14
  116.6 0.2 fusion.17
  116.9 0.3 copy.43
  117.1 0.8 copy.44
  118.0 0.0 copy-done.9
  118.0 0.0 copy-done.10
  118.0 2.1 %multiply_convert_fusion = bf16[2,33,16,5,128]{4,2,3,1,0:T(8,128)(2,1)} fusion(bf16[5,128,512,1,1]{2,1,0,4,3:T(8,128)(2,1)S(1)} %bitcast.104, f32[33,16]{1,0:T(8,128)S(1)} %add_rsqrt_fusion, bf16[1,33,16,512]{3,2,1,0:T(8,128)(2,1)S(1)} %copy-done.10, bf16[1,33,16,512]{3,2,1,0:T(8,128)(2,1)S(1)} %copy-done.9), kind=kOutput, calls=%fused_computation.2 | convolution fusion | flops 695574528 | bytes 3090496 | tf_op jit(solution)/shard_map/dot_general | solution.py:91
  (7 shorter events, 0.1 us)
Async XLA Ops:
  0.6 22.2 %copy-start = (f32[8,64,64]{2,1,0:T(8,128)S(1)}, f32[8,64,64]{2,1,0:T(8,128)}, u32[]{:S(2)}) copy-start(f32[8,64,64]{2,1,0:T(8,128)} %param.7) | copy-start | bytes 393220
  6.0 12.6 %copy-start.6 = (bf16[2,33,16,5,128]{4,2,3,1,0:T(8,128)(2,1)S(1)}, bf16[2,33,16,5,128]{4,2,3,1,0:T(8,128)(2,1)}, u32[]{:S(2)}) copy-start(bf16[2,33,16,5,128]{4,2,3,1,0:T(8,128)(2,1)} %param.6) | copy-start | bytes 4055044
  11.3 24.0 %all-to-all-start = ((bf16[16,2,10240]{2,1,0:T(2,128)(2,1)}), bf16[16,2,10240]{2,1,0:T(2,128)(2,1)S(1)}, u32[]{:S(2)}, u32[]{:S(2)}) async-start(bf16[16,2,10240]{2,1,0:T(2,128)(2,1)} %reshape.176), calls=%async_computation | async-start | bytes 1310720 | tf_op jit(solution)/shard_map/all_to_all | solution.py:46
  20.8 2.0 %copy-start.8 = (s32[2]{0:T(128)S(1)}, s32[2]{0:T(128)}, u32[]{:S(2)}) copy-start(s32[2]{0:T(128)} %param.8) | copy-start | bytes 28
  21.1 2.1 %copy-start.7 = (s32[8]{0:T(128)S(1)}, s32[8]{0:T(128)}, u32[]{:S(2)}) copy-start(s32[8]{0:T(128)} %param.9) | copy-start | bytes 100
  43.6 1.9 %copy-start.1 = (bf16[32,5,16,128]{3,1,0,2:T(8,128)(2,1)}, bf16[32,5,16,128]{3,1,0,2:T(8,128)(2,1)S(1)}, u32[]{:S(2)}) copy-start(bf16[32,5,16,128]{3,1,0,2:T(8,128)(2,1)S(1)} %copy.36) | copy-start | bytes 1966084
  53.6 1.1 copy-start.5
  54.3 1.1 copy-start.4
  55.9 1.1 copy-start.3
  107.9 2.4 %copy-start.2 = (bf16[32,5,16,128]{3,1,0,2:T(8,128)(2,1)S(1)}, bf16[32,5,16,128]{3,1,0,2:T(8,128)(2,1)}, u32[]{:S(2)}) copy-start(bf16[32,5,16,128]{3,1,0,2:T(8,128)(2,1)} %copy-done.1) | copy-start | bytes 1966084
  116.5 1.5 %copy-start.9 = (bf16[1,33,16,512]{3,2,1,0:T(8,128)(2,1)S(1)}, bf16[1,33,16,512]{3,2,1,0:T(8,128)(2,1)}, u32[]{:S(2)}) copy-start(bf16[1,33,16,512]{3,2,1,0:T(8,128)(2,1)} %fusion.11) | copy-start | bytes 1622020
  116.5 1.5 %copy-start.10 = (bf16[1,33,16,512]{3,2,1,0:T(8,128)(2,1)S(1)}, bf16[1,33,16,512]{3,2,1,0:T(8,128)(2,1)}, u32[]{:S(2)}) copy-start(bf16[1,33,16,512]{3,2,1,0:T(8,128)(2,1)} %fusion.10) | copy-start | bytes 1622020
where the time goes:
time: 121 us; the launch traced here: 120 us
  blocking collectives  48.1 us (40%)
  local copies, waits for them, and re-layouts  30.1 us (25%)
  matrix products  21.4 us (18%)
  waiting for transfers between devices  9.49 us (8%)
  starting transfers between devices  7.39 us (6%)
  other arithmetic  2.59 us (2%)
    psum x1, blocking collectives, on_device(): lax.psum((coeff_part, gram_real, gram_imag), ('tm', 'space'))  48.1 us
    unnamed x27, local copies, waits for them, and re-layouts  15.7 us
    all_to_all x1, waiting for transfers between devices, on_device(): lax.all_to_all(snapshots, 'tm', split_axis=2, concat_axis=0, tiled=True)  9.49 us
    all_to_all x1, starting transfers between devices, on_device(): lax.all_to_all(snapshots, 'tm', split_axis=2, concat_axis=0, tiled=True)  7.39 us
    all_to_all x1, local copies, waits for them, and re-layouts, on_device(): lax.all_to_all(snapshots, 'tm', split_axis=2, concat_axis=0, tiled=True)  4.46 us
    dot_general x1, matrix products, apply_mass(): jnp.einsum('...ep,epq->...eq', shaped, local_mass, precision=lax.Precisio...  3.49 us
    another operation x1, local copies, waits for them, and re-layouts, apply_mass(): shaped = field.reshape(lead + (elem_count, local_mass.shape[1]))  3.11 us
    dot_general x1, matrix products, on_device(): jnp.einsum('fbt,fbk->fkt', table_float[1], coeff_round[1])  3.02 us
  transfers between devices with their start and end apart: 1, of which 1 were waited for; matrix products, arithmetic and copies ran while one was open for 6% of the time, Pallas kernels for 0%

commit v1 on v0

--- a/solution.py
+++ b/solution.py
@@ -5,6 +5,11 @@
 from jax.sharding import PartitionSpec as P
 
 NT = 256
+
+
+def replace_slices_here(row_data):
+    parts_out = lax.psum(lax.psum(row_data, axis_name="space"), axis_name="tm")
+    return parts_out
 
 
 def spectral_table(offsets, window_len, freq_count, record_len):
@@ -73,7 +78,7 @@
     coeff_part = jnp.stack([coeff_real, coeff_imag])
     spec_round = spectra.astype(jnp.bfloat16).reshape(2, freq_count, block_total, flat_len)
     gram_real, gram_imag = paired_einsum("fbx,fcx->fbc", spec_round, weighted)
-    coeff_sum, gram_real, gram_imag = lax.psum((coeff_part, gram_real, gram_imag), ("tm", "space"))
+    coeff_sum, gram_real, gram_imag = replace_slices_here((coeff_part, gram_real, gram_imag))
     coeffs = coeff_sum / math.sqrt(entries)
     table_float = dft_table.astype(jnp.float32)
     coeff_round = lax.optimization_barrier(coeffs.astype(jnp.bfloat16)).astype(jnp.float32)

time: 121 us -> 156 us (1.29)
  blocking collectives: 48.1 us -> 84.1 us
    psum x1 -> x2, blocking collectives: 48.1 us -> 84.1 us  [replace_slices_here(): parts_out = lax.psum(lax.psum(row_data, axis_name='space'), axis_name='tm')]
    unnamed x27 -> x25, local copies, waits for them, and re-layouts: 15.7 us -> 15.8 us
  transfers between devices with their start and end apart: 1 -> 1, of which waited for: 1 -> 1; matrix products, arithmetic and copies ran while one was open for 6% -> 5% of each run, Pallas kernels for 0% -> 0%
where the time goes in v1:
time: 156 us; the launch traced here: 155 us
  blocking collectives  84.1 us (54%)
  local copies, waits for them, and re-layouts  30.2 us (19%)
  matrix products  20.7 us (13%)
  waiting for transfers between devices  9.49 us (6%)
  starting transfers between devices  7.39 us (5%)
  other arithmetic  2.59 us (2%)
    psum x2, blocking collectives, replace_slices_here(): parts_out = lax.psum(lax.psum(row_data, axis_name='space'), axis_name='tm')  84.1 us
    unnamed x25, local copies, waits for them, and re-layouts  15.8 us
    all_to_all x1, waiting for transfers between devices, on_device(): lax.all_to_all(snapshots, 'tm', split_axis=2, concat_axis=0, tiled=True)  9.49 us
    all_to_all x1, starting transfers between devices, on_device(): lax.all_to_all(snapshots, 'tm', split_axis=2, concat_axis=0, tiled=True)  7.39 us
    all_to_all x1, local copies, waits for them, and re-layouts, on_device(): lax.all_to_all(snapshots, 'tm', split_axis=2, concat_axis=0, tiled=True)  4.46 us
    dot_general x1, matrix products, apply_mass(): jnp.einsum('...ep,epq->...eq', shaped, local_mass, precision=lax.Precisio...  3.49 us
  transfers between devices with their start and end apart: 1, of which 1 were waited for; matrix products, arithmetic and copies ran while one was open for 5% of the time, Pallas kernels for 0%

profile of v1, /device:TPU:0, one launch (start us, length us, event | category | flops | bytes accessed | tf_op | source)
XLA Modules:
  0.0 155.4 jit_solution(7317628550784300448)
XLA Ops:
  0.6 0.0 copy-start
  0.6 5.4 %copy.35 = bf16[32,5,2048]{0,1,2:T(8,128)(2,1)} copy(bf16[32,5,2048]{2,0,1:T(8,128)(2,1)} %param.5) | data formatting | bytes 1310720 | tf_op args[0]
  6.0 5.2 %reshape.176 = bf16[16,2,10240]{2,1,0:T(2,128)(2,1)} reshape(bf16[2048,5,32]{2,1,0:T(8,128)(2,1)} %bitcast.99) | data formatting | bytes 1310720
  11.3 7.4 %all-to-all-start = ((bf16[16,2,10240]{2,1,0:T(2,128)(2,1)}), bf16[16,2,10240]{2,1,0:T(2,128)(2,1)S(1)}, u32[]{:S(2)}, u32[]{:S(2)}) async-start(bf16[16,2,10240]{2,1,0:T(2,128)(2,1)} %reshape.176), calls=%async_computation | async-start | bytes 1310720 | tf_op jit(solution)/shard_map/all_to_all | solution.py:51
  18.7 0.0 copy-done.6
  18.7 0.2 fusion.69
  18.9 0.3 copy.40
  19.2 1.6 %squeeze.25 = bf16[33,16,640]{2,1,0:T(8,128)(2,1)} reshape(bf16[1,33,16,5,128]{4,3,2,1,0:T(8,128)(2,1)S(1)} %copy.40) | data formatting | bytes 1351680 | tf_op jit(solution)/shard_map/squeeze | solution.py:42
  20.8 0.3 copy.42
  21.1 0.0 copy-start.7
  21.1 1.7 %squeeze.27 = bf16[33,16,640]{2,1,0:T(8,128)(2,1)} reshape(bf16[1,33,16,5,128]{4,3,2,1,0:T(8,128)(2,1)S(1)} %copy.42) | data formatting | bytes 1351680 | tf_op jit(solution)/shard_map/squeeze | solution.py:43
  22.8 0.0 copy-done
  22.8 0.0 copy-done.8
  22.8 0.4 convolution_bitcast_fusion
  23.2 0.0 copy-done.7
  23.2 0.1 fusion.42
  23.3 0.1 multiply_select_fusion
  23.5 2.2 %multiply_convert_fusion.2 = (bf16[1,33,8,512]{3,2,1,0:T(8,128)(2,1)S(1)}, bf16[1,33,8,512]{3,2,1,0:T(8,128)(2,1)S(1)}) fusion(s32[8,512]{1,0:T(8,128)S(1)} %fusion.42, f32[8,512]{1,0:T(8,128)S(1)} %get-tuple-element.24, f32[8,512]{1,0:T(8,128)S(1)} %get-tuple-element.25), kind=kLoop, calls=%fused_computation.38 | loop fusion | flops 2433024 | bytes 589824 | tf_op jit(solution)/shard_map/slice | solution.py:85
  25.7 0.1 pad_maximum_fusion
  25.7 9.5 %all-to-all-done = bf16[16,2,10240]{2,1,0:T(2,128)(2,1)S(1)} async-done(((bf16[16,2,10240]{2,1,0:T(2,128)(2,1)}), bf16[16,2,10240]{2,1,0:T(2,128)(2,1)S(1)}, u32[]{:S(2)}, u32[]{:S(2)}) %all-to-all-start) | async-done | bytes 655392 | tf_op jit(solution)/shard_map/all_to_all | solution.py:51
  35.2 4.0 %reshape.177 = bf16[2048,5,32]{2,1,0:T(8,128)(2,1)} reshape(bf16[16,2,10240]{2,1,0:T(2,128)(2,1)S(1)} %all-to-all-done) | data formatting | bytes 1310720
  39.2 4.5 %copy.36 = bf16[32,5,16,128]{3,1,0,2:T(8,128)(2,1)S(1)} copy(bf16[32,5,16,128]{0,1,3,2:T(8,128)(2,1)} %bitcast.98) | data formatting | bytes 1310720 | tf_op jit(solution)/shard_map/all_to_all | solution.py:51
  43.7 0.0 copy-start.1
  43.7 1.9 %fusion.70 = (bf16[528,640]{1,0:T(8,128)(2,1)}, f32[528,640]{1,0:T(8,128)}) fusion(bf16[528,512]{1,0:T(8,128)(2,1)S(1)} %bitcast.103, bf16[64,8,5,128]{3,2,1,0:T(8,128)(2,1)S(1)} %bitcast.100), kind=kOutput, calls=%fused_computation.95 | convolution fusion | flops 346368000 | bytes 3223552 | tf_op jit(solution)/shard_map/dot_general | solution.py:61
  45.6 0.0 copy-done.1
  45.6 3.1 %reshape_reshape.3 = f32[2,33,8,5,2,64]{5,4,3,2,1,0:T(2,128)S(1)} reshape(f32[528,640]{1,0:T(8,128)} %get-tuple-element.27) | data formatting | bytes 2703360 | tf_op jit(solution)/shard_map/reshape;reshape | solution.py:35
  48.7 3.5 %fusion.5 = bf16[2,33,8,5,2,64]{5,1,3,2,0,4:T(8,128)(2,1)S(1)} fusion(f32[2,33,8,5,2,64]{5,4,3,2,1,0:T(2,128)S(1)} %reshape_reshape.3, f32[2,64,64,1,1,1]{2,0,1,5,4,3:T(2,128)S(1)} %convolution_bitcast_fusion), kind=kOutput, calls=%fused_computation.4 | convolution fusion | flops 259860480 | bytes 2060288 | tf_op jit(solution)/shard_map/...ep,epq->...eq/dot_general | solution.py:36
  52.2 0.3 fusion.68
  52.5 0.7 copy.41
  53.2 0.4 squeeze.26
  53.6 0.0 copy-start.5
  53.6 0.7 copy.39
  54.4 0.0 copy-start.4
  54.4 0.4 squeeze.24
  54.8 0.0 copy-done.5
  54.8 0.3 fusion.36
  55.1 0.3 fusion.37
  55.4 0.1 copy-done.4
  55.5 0.4 fusion.71
  55.9 0.0 copy-start.3
  55.9 0.4 fusion.72
  56.3 0.4 convolution_subtract_fusion.1
  56.6 0.3 convolution_add_fusion.1
  56.9 0.1 copy-done.3
  57.0 0.3 fusion.16
  57.3 0.4 fusion.15
  57.7 17.8 %all-reduce.1 = (f32[2,33,8,16]{3,2,1,0:T(8,128)S(1)}, f32[33,8,8]{2,1,0:T(8,128)S(1)}, f32[33,8,8]{2,1,0:T(8,128)S(1)}) all-reduce(f32[2,33,8,16]{3,2,1,0:T(8,128)S(1)} %pad_maximum_fusion.1, f32[33,8,8]{2,1,0:T(8,128)S(1)} %convolution_add_fusion.1, ...), channel_id=1, replica_groups=mesh['tm'=16,'space'=2] {'space'}, use_global_device_ids=true, to_apply=%region_0.1 | all-reduce | flops 12672 | bytes 101376 | tf_op jit(solution)/shard_map/psum | solution.py:11
  75.5 66.3 %all-reduce = (f32[2,33,8,16]{3,2,1,0:T(8,128)S(1)}, bf16[33,8,8]{2,1,0:T(8,128)(2,1)S(1)}, bf16[33,8,8]{2,1,0:T(8,128)(2,1)S(1)}) all-reduce(f32[2,33,8,16]{3,2,1,0:T(8,128)S(1)} %get-tuple-element.13, f32[33,8,8]{2,1,0:T(8,128)S(1)} %get-tuple-element.14, ...), channel_id=1, replica_groups=mesh['tm'=16,'space'=2] {'tm'}, use_global_device_ids=true, to_apply=%region_1.2 | all-reduce | flops 12672 | bytes 92928 | tf_op jit(solution)/shard_map/psum | solution.py:11
  141.9 2.0 %fusion.33 = f32[33,16,512]{2,1,0:T(8,128)S(1)} fusion(s32[8,512]{1,0:T(8,128)S(1)} %fusion.42, f32[8,512]{1,0:T(8,128)S(1)} %get-tuple-element.24, bf16[2,33,8,16]{3,2,1,0:T(8,128)(2,1)S(1)} %get-tuple-element.20), kind=kOutput, calls=%fused_computation.50 | convolution fusion | flops 6488064 | bytes 1181696 | tf_op jit(solution)/shard_map/fbt,fbk->fkt/dot_general | solution.py:85
  143.9 0.0 copy-start.2
  143.9 2.0 %fusion.31 = f32[33,16,512]{2,1,0:T(8,128)S(1)} fusion(s32[8,512]{1,0:T(8,128)S(1)} %fusion.42, f32[8,512]{1,0:T(8,128)S(1)} %get-tuple-element.24, bf16[2,33,8,16]{3,2,1,0:T(8,128)(2,1)S(1)} %get-tuple-element.20), kind=kOutput, calls=%fused_computation.48 | convolution fusion | flops 6488064 | bytes 1181696 | tf_op jit(solution)/shard_map/fbt,fbk->fkt/dot_general | solution.py:88
  146.0 0.2 fusion.39
  146.1 0.2 fusion.40
  146.3 0.0 copy-done.2
  146.3 0.1 copy.68
  146.5 2.3 %fusion.11 = bf16[1,33,16,512]{3,2,1,0:T(8,128)(2,1)S(1)} fusion(f32[33,16,512]{2,1,0:T(8,128)S(1)} %fusion.33, f32[8,512]{1,0:T(8,128)S(1)} %get-tuple-element.25, s32[8,512]{1,0:T(8,128)S(1)} %fusion.42, bf16[2,33,8,16]{3,2,1,0:T(8,128)(2,1)S(1)} %get-tuple-element.20), kind=kOutput, calls=%fused_computation.10 | convolution fusion | flops 7028736 | bytes 1722368 | tf_op jit(solution)/shard_map/fbt,fbk->fkt/dot_general | solution.py:85
  148.8 3.0 %fusion.10 = bf16[1,33,16,512]{3,2,1,0:T(8,128)(2,1)} fusion(f32[33,16,512]{2,1,0:T(8,128)S(1)} %fusion.31, f32[8,512]{1,0:T(8,128)S(1)} %get-tuple-element.25, s32[8,512]{1,0:T(8,128)S(1)} %fusion.42, bf16[2,33,8,16]{3,2,1,0:T(8,128)(2,1)S(1)} %get-tuple-element.20), kind=kOutput, calls=%fused_computation.9 | convolution fusion | flops 7028736 | bytes 1722368 | tf_op jit(solution)/shard_map/fbt,fbk->fkt/dot_general | solution.py:88
  151.8 0.0 copy-start.9
  151.8 0.2 fusion.14
  151.9 0.2 fusion.17
  152.2 0.3 copy.43
  152.4 0.8 copy.44
  153.3 0.0 copy-done.9
  153.3 2.1 %multiply_convert_fusion = bf16[2,33,16,5,128]{4,2,3,1,0:T(8,128)(2,1)} fusion(bf16[5,128,512,1,1]{2,1,0,4,3:T(8,128)(2,1)S(1)} %bitcast.104, f32[33,16]{1,0:T(8,128)S(1)} %add_rsqrt_fusion, bf16[1,33,16,512]{3,2,1,0:T(8,128)(2,1)S(1)} %copy-done.9, bf16[1,33,16,512]{3,2,1,0:T(8,128)(2,1)S(1)} %fusion.11), kind=kOutput, calls=%fused_computation.2 | convolution fusion | flops 695574528 | bytes 3090496 | tf_op jit(solution)/shard_map/dot_general | solution.py:96
  (6 shorter events, 0.1 us)
Async XLA Ops:
  0.6 22.2 %copy-start = (f32[8,64,64]{2,1,0:T(8,128)S(1)}, f32[8,64,64]{2,1,0:T(8,128)}, u32[]{:S(2)}) copy-start(f32[8,64,64]{2,1,0:T(8,128)} %param.7) | copy-start | bytes 393220
  6.0 12.6 %copy-start.6 = (bf16[2,33,16,5,128]{4,2,3,1,0:T(8,128)(2,1)S(1)}, bf16[2,33,16,5,128]{4,2,3,1,0:T(8,128)(2,1)}, u32[]{:S(2)}) copy-start(bf16[2,33,16,5,128]{4,2,3,1,0:T(8,128)(2,1)} %param.6) | copy-start | bytes 4055044
  11.3 24.0 %all-to-all-start = ((bf16[16,2,10240]{2,1,0:T(2,128)(2,1)}), bf16[16,2,10240]{2,1,0:T(2,128)(2,1)S(1)}, u32[]{:S(2)}, u32[]{:S(2)}) async-start(bf16[16,2,10240]{2,1,0:T(2,128)(2,1)} %reshape.176), calls=%async_computation | async-start | bytes 1310720 | tf_op jit(solution)/shard_map/all_to_all | solution.py:51
  20.8 2.0 %copy-start.8 = (s32[2]{0:T(128)S(1)}, s32[2]{0:T(128)}, u32[]{:S(2)}) copy-start(s32[2]{0:T(128)} %param.8) | copy-start | bytes 28
  21.1 2.1 %copy-start.7 = (s32[8]{0:T(128)S(1)}, s32[8]{0:T(128)}, u32[]{:S(2)}) copy-start(s32[8]{0:T(128)} %param.9) | copy-start | bytes 100
  43.7 1.9 %copy-start.1 = (bf16[32,5,16,128]{3,1,0,2:T(8,128)(2,1)}, bf16[32,5,16,128]{3,1,0,2:T(8,128)(2,1)S(1)}, u32[]{:S(2)}) copy-start(bf16[32,5,16,128]{3,1,0,2:T(8,128)(2,1)S(1)} %copy.36) | copy-start | bytes 1966084
  53.6 1.1 copy-start.5
  54.4 1.1 copy-start.4
  55.9 1.1 copy-start.3
  143.9 2.4 %copy-start.2 = (bf16[32,5,16,128]{3,1,0,2:T(8,128)(2,1)S(1)}, bf16[32,5,16,128]{3,1,0,2:T(8,128)(2,1)}, u32[]{:S(2)}) copy-start(bf16[32,5,16,128]{3,1,0,2:T(8,128)(2,1)} %copy-done.1) | copy-start | bytes 1966084
  151.8 1.5 copy-start.9
